TPU v7x, 32 devices: a whole 2x2x4 slice. The times are simulated.
32 devices in a mesh: gx: 4 (over z), gy: 8 (over y, x, core).
Axes of the slice: x: 2, y: 2, z: 4, core: 2. Of those that a mesh axis runs over, the one named last changes fastest.
Arguments:
- point_feats: bfloat16 [512, 64, 128], P(('gx', 'gy')), may hold values from -6 to 6
- offsets: bfloat16 [512, 3, 128], P(('gx', 'gy')), may hold values from 0 to 1
- targets: int32 [512, 1], P(('gx', 'gy')), may hold values from 0 to 7; in each aligned block of 16 rows (0 to 15, 16 to 31, ...) at most 4 rows name the same one
- zstart: int32 [512], P(('gx', 'gy')), may hold values from 0 to 63
- enc_in: float32 [3, 64], replicated, may hold values from -4 to 4
- enc_bias: float32 [64], replicated, may hold values from -4 to 4
- enc_out: bfloat16 [64, 64], replicated, may hold values from -0.75 to 0.75
- dec_in: float32 [3, 64], replicated, may hold values from -4 to 4
- dec_bias: float32 [64], replicated, may hold values from -4 to 4
- dec_out: bfloat16 [64, 64], replicated, may hold values from -0.75 to 0.75
- spec_weight: float32 [32, 32, 32, 4096], P(None, 'gx', 'gy'), may hold values from -0.75 to 0.75
- local_weight: float32 [64, 64], replicated, may hold values from -0.75 to 0.75
- local_bias: float32 [64], replicated, may hold values from -3 to 3
- head_weight: float32 [64], replicated, may hold values from -4 to 4
Outputs:
- pressure: float32 [512, 128], P(('gx', 'gy'))
Inputs may be any that keep to these rules, and one draw needn't show every extreme that they name: `targets`: A block's cells lie in the pencil of its own gx row with this gy index; at most 4 blocks of one device share a target, and exactly 4 do on some devices.
All inputs are finite; a program needn't handle non-finite values.
Results may differ from a plain program's by a relative error of at most 0.0014.
Values may be sent and summed in bfloat16 or wider, within the bound.
No kernel may reach another device: no remote copies, remote signals or barrier semaphores. Data moves between devices by JAX's collectives and lax.ppermute only.
A program may use at most 128 MiB of HBM per device.

v0:
```python
import jax
import jax.numpy as jnp
from jax import lax
from jax.sharding import PartitionSpec as P

G = 64
M = 32
kernel_spread = 2.0
highest = lax.Precision.HIGHEST


def real_basis(length, modes):
    half = modes // 2
    places = jnp.arange(length).astype(jnp.float32)
    frequency = jnp.arange(half).astype(jnp.float32)
    angle_cos = 2.0 * jnp.pi * frequency[:, None] * places[None, :] / length
    angle_sin = 2.0 * jnp.pi * (frequency[:, None] + 1.0) * places[None, :] / length
    table = jnp.concatenate([jnp.cos(angle_cos), jnp.sin(angle_sin)], 0)
    return table * jnp.float32((2.0 / length) ** 0.5)


def tile_terms(offset_rows, weight_in, bias_in, cells_x, cells_y):
    offset_rows = offset_rows.astype(jnp.float32)
    cell_ids = jnp.arange(cells_x * cells_y)
    center_x = (cell_ids // cells_y).astype(jnp.float32) + 0.5
    center_y = (cell_ids % cells_y).astype(jnp.float32) + 0.5
    delta_x = (center_x[None, :, None] - cells_x * offset_rows[:, 0][:, None, :]) / kernel_spread
    delta_y = (center_y[None, :, None] - cells_y * offset_rows[:, 1][:, None, :]) / kernel_spread
    delta_z = (0.5 - offset_rows[:, 2][:, None, :]) / kernel_spread
    closeness = jnp.exp(-0.5 * (delta_x * delta_x + delta_y * delta_y + delta_z * delta_z))
    before = (
        delta_x[..., None] * weight_in[0]
        + delta_y[..., None] * weight_in[1]
        + delta_z[..., None] * weight_in[2]
        + bias_in
    )
    return (jax.nn.gelu(before, approximate=False) * closeness[..., None]).astype(jnp.bfloat16)


def encode(weighted, feats, out_weight):
    partial_sums = jnp.einsum("bcph,bop->bcho", weighted, feats, preferred_element_type=jnp.float32)
    return jnp.einsum(
        "bcho,ho->boc", partial_sums, out_weight.astype(jnp.float32), precision=highest
    ) * feats.shape[2] ** (-0.5)


def decode(weighted, tile_values, out_weight):
    folded = (
        out_weight.astype(jnp.float32)[None, None, :, :]
        * jnp.transpose(tile_values.astype(jnp.float32), (0, 2, 1))[:, :, None, :]
    ).astype(jnp.bfloat16)
    return jnp.einsum(
        "bcph,bcho->bop", weighted, folded, preferred_element_type=jnp.float32
    ) * weighted.shape[1] ** (-0.5)


def run_groups(function, arrays, row_count):
    group_size = 8
    shaped = tuple(
        (
            member.reshape((row_count // group_size, group_size) + member.shape[1:])
            for member in arrays
        )
    )
    result = lax.map(function, shaped)
    return result.reshape((row_count,) + result.shape[2:])


def fourier(pencil, spec_weight, local_weight, local_bias, table):
    channels = pencil.shape[0]
    spectrum = jnp.einsum("oxyz,kz->oxyk", pencil, table, precision=highest)
    spectrum = lax.all_to_all(
        spectrum.astype(jnp.bfloat16), "gy", split_axis=3, concat_axis=2, tiled=True
    ).astype(spectrum.dtype)
    spectrum = jnp.einsum("oxyk,ly->oxlk", spectrum, table, precision=highest)
    spectrum = lax.all_to_all(spectrum, "gx", split_axis=2, concat_axis=1, tiled=True)
    spectrum = jnp.einsum("oxlk,jx->ojlk", spectrum, table, precision=highest)
    mode_weight = spec_weight.reshape(spec_weight.shape[:3] + (channels, channels))
    mixed_modes = jnp.einsum("ojlk,jlkoq->qjlk", spectrum, mode_weight, precision=highest)
    returned = jnp.einsum("ojlk,jx->oxlk", mixed_modes, table, precision=highest)
    returned = lax.all_to_all(
        returned.astype(jnp.bfloat16), "gx", split_axis=1, concat_axis=2, tiled=True
    ).astype(returned.dtype)
    returned = jnp.einsum("oxlk,ly->oxyk", returned, table, precision=highest)
    returned = lax.all_to_all(
        returned.astype(jnp.bfloat16), "gy", split_axis=2, concat_axis=3, tiled=True
    ).astype(returned.dtype)
    returned = jnp.einsum("oxyk,kz->oxyz", returned, table, precision=highest)
    local_term = (
        jnp.einsum("oxyz,oq->qxyz", pencil, local_weight, precision=highest)
        + local_bias[:, None, None, None]
    )
    return jax.nn.gelu(returned + local_term, approximate=False).astype(jnp.bfloat16)


def local(
    point_feats,
    offsets,
    targets,
    zstart,
    enc_in,
    enc_bias,
    enc_out,
    dec_in,
    dec_bias,
    dec_out,
    spec_weight,
    local_weight,
    local_bias,
    head_weight,
):
    rows_count = lax.axis_size("gx")
    cols_count = lax.axis_size("gy")
    cells_x = G // rows_count
    cells_y = G // cols_count
    tile_cells = cells_x * cells_y
    block_count = point_feats.shape[0]
    channels = point_feats.shape[1]
    capacity = max(2, 2 * block_count // cols_count)
    slot_count = cols_count * capacity
    target = targets[:, 0]
    onehot = (target[:, None] == jnp.arange(cols_count)[None, :]).astype(jnp.int32)
    slot_rank = jnp.sum(onehot * (jnp.cumsum(onehot, axis=0) - onehot), axis=1)
    slot_of = target * capacity + slot_rank
    placement = jnp.arange(slot_count)[:, None] == slot_of[None, :]
    place_float = placement.astype(jnp.float32)
    place_half = placement.astype(jnp.bfloat16)
    planes_sent = jnp.dot(place_float, zstart.astype(jnp.float32), precision=highest)
    table = real_basis(G, M)

    def encode_rows(pieces):
        feats_group, offs_group = pieces
        weighted = tile_terms(offs_group, enc_in, enc_bias, cells_x, cells_y)
        return encode(weighted, feats_group, enc_out)

    def decode_rows(pieces):
        tiles_group, offs_group = pieces
        weighted = tile_terms(offs_group, dec_in, dec_bias, cells_x, cells_y)
        values = decode(weighted, tiles_group, dec_out)
        return jnp.einsum(
            "bop,o->bp", jax.nn.gelu(values, approximate=False), head_weight, precision=highest
        )

    own_terms = run_groups(encode_rows, (point_feats, offsets), block_count)
    send_terms = jnp.einsum("sb,boc->soc", place_float, own_terms, precision=highest)
    got_terms, got_planes = (
        lax.all_to_all(
            send_terms.reshape(cols_count, capacity, channels, tile_cells),
            "gy",
            split_axis=0,
            concat_axis=0,
            tiled=True,
        ),
        lax.all_to_all(
            planes_sent.reshape(cols_count, capacity), "gy", split_axis=0, concat_axis=0, tiled=True
        ),
    )
    contrib = got_terms.reshape(slot_count, channels, tile_cells)
    planes_got = got_planes.reshape(slot_count)
    plane_table = planes_got[:, None] == jnp.arange(G).astype(jnp.float32)[None, :]
    pencil = jnp.einsum("soc,sz->ocz", contrib, plane_table.astype(jnp.float32), precision=highest)
    pencil = pencil.reshape(channels, cells_x, cells_y, G)
    latent = fourier(pencil, spec_weight, local_weight, local_bias, table).reshape(
        channels, tile_cells, G
    )
    tile_values = jnp.einsum(
        "ocz,sz->soc", latent, plane_table.astype(jnp.bfloat16), preferred_element_type=jnp.float32
    ).astype(jnp.bfloat16)
    returned = lax.all_to_all(
        tile_values.reshape(cols_count, capacity, channels, tile_cells),
        "gy",
        split_axis=0,
        concat_axis=0,
        tiled=True,
    )
    returned = returned.reshape(slot_count, channels, tile_cells)
    own_tiles = jnp.einsum(
        "sb,soc->boc", place_half, returned, preferred_element_type=jnp.float32
    ).astype(jnp.bfloat16)
    return run_groups(decode_rows, (own_tiles, offsets), block_count)


def solution(mesh):
    placed = (
        P(("gx", "gy"), None, None),
        P(("gx", "gy"), None, None),
        P(("gx", "gy"), None),
        P(("gx", "gy")),
        P(),
        P(),
        P(),
        P(),
        P(),
        P(),
        P(None, "gx", "gy", None),
        P(),
        P(),
        P(),
    )
    return jax.shard_map(
        local, mesh=mesh, in_specs=placed, out_specs=P(("gx", "gy"), None), check_vma=False
    )
```

profile of v0, /device:TPU:0, one launch (start us, length us, event | category | flops | bytes accessed | tf_op | source)
XLA Modules:
  0.0 560.5 jit_solution(12473694886595939378)
XLA Ops:
  0.0 0.7 fusion.316
  0.8 0.8 select_reduce_fusion
  1.6 0.7 multiply_add_fusion.1
  2.8 0.8 convolution_bitcast_fusion.2
  3.7 0.7 all_to_all.64
  4.4 5.2 all-to-all-start
  10.1 1.3 copy.59
  11.5 179.2 %while.24 = (s32[]{:T(128)}, f32[2,8,64,128]{3,2,1,0:T(8,128)}, bf16[2,8,3,128]{3,1,2,0:T(8,128)(2,1)}, f32[3,64]{1,0:T(4,128)}, f32[64]{0:T(128)}, /*index=5*/b...) while((s32[]{:T(128)}, f32[2,8,64,128]{3,2,1,0:T(8,128)}, bf16[2,8,3,128]{3,1,2,0:T(8,128)(2,1)}, ...), condition=%wide.region_3.4_spmd, body=%wide.region_2.3_spmd.sunk | while | flops 1678981120 | bytes 9416085 | solution.py:65
  11.5 0.7 bitcast_convert_fusion.7
  12.5 0.8 slice_bitcast_fusion.8
  13.3 0.7 bitcast_convert_fusion.6
  14.1 85.9 %multiply_reduce_fusion.2 = f32[64,8,128]{0,2,1:T(8,128)S(1)} fusion(f32[64,64]{0,1:T(8,128)S(1)} %bitcast_convert_fusion.6, f32[8,128,128]{2,1,0:T(8,128)S(1)} %get-tuple-element.435, f32[64]{0:T(128)} %get-tuple-element.482, f32[8,128,64]{1,2,0:T(8,128)S(1)} %broadcast_multiply_fusion.4, f32[64]{0:T(128)S(1)} %get-tuple-element.438, ...), kind=kOutput, calls=%fused_computation.219.clone.3 | convolution fusion | flops 1677656064 | bytes 2246144 | tf_op jit(solution)/shard_map/while/body/eval_jaxpr/bcph,bop->bcho/dot_general | solution.py:41
  100.2 0.8 copy-done.3
  101.0 0.7 bitcast_convert_fusion.7
  102.0 0.8 slice_bitcast_fusion.8
  102.9 0.7 bitcast_convert_fusion.6
  103.6 85.9 %multiply_reduce_fusion.2 = f32[64,8,128]{0,2,1:T(8,128)S(1)} fusion(f32[64,64]{0,1:T(8,128)S(1)} %bitcast_convert_fusion.6, f32[8,128,128]{2,1,0:T(8,128)S(1)} %get-tuple-element.435, f32[64]{0:T(128)} %get-tuple-element.482, f32[8,128,64]{1,2,0:T(8,128)S(1)} %broadcast_multiply_fusion.4, f32[64]{0:T(128)S(1)} %get-tuple-element.438, ...), kind=kOutput, calls=%fused_computation.219.clone.3 | convolution fusion | flops 1677656064 | bytes 2246144 | tf_op jit(solution)/shard_map/while/body/eval_jaxpr/bcph,bop->bcho/dot_general | solution.py:41
  189.7 0.8 copy-done.3
  190.7 1.8 fusion.300
  192.5 1.2 copy.61
  193.7 4.2 all-to-all-start.1
  198.6 1.3 reduce.5
  200.0 13.3 %all-to-all-done.1 = f32[8,4,64,128]{3,2,1,0:T(8,128)S(1)} async-done(((f32[8,4,64,128]{3,2,1,0:T(8,128)}), f32[8,4,64,128]{3,2,1,0:T(8,128)S(1)}, u32[]{:S(2)}, u32[]{:S(2)}) %all-to-all-start.1) | async-done | bytes 1048608 | tf_op jit(solution)/shard_map/all_to_all | solution.py:147
  213.3 1.8 copy.62
  215.1 3.5 fusion.309
  218.7 2.1 copy-done.1
  220.7 11.4 %convolution_convert_fusion.1 = bf16[64,16,8,32]{0,3,2,1:T(8,128)(2,1)S(1)} fusion(f32[64,16,8,64]{3,0,2,1:T(8,128)S(1)} %fusion.309, f32[16,64]{1,0:T(8,128)S(1)} %get-tuple-element.319, f32[16,64]{1,0:T(8,128)S(1)} %get-tuple-element.318), kind=kOutput, calls=%fused_computation.359 | convolution fusion | flops 201592832 | bytes 2629632 | tf_op jit(solution)/shard_map/oxyz,kz->oxyk/dot_general | solution.py:71
  232.6 0.9 reshape.239
  233.5 12.1 %all_to_all.91 = bf16[8,2,16384]{2,1,0:T(2,128)(2,1)S(1)} all-to-all(bf16[8,2,16384]{2,1,0:T(2,128)(2,1)S(1)} %reshape.239), channel_id=1, replica_groups=mesh['gx'=4,'gy'=8] {'gy'}, dimensions={0} | all-to-all | bytes 1048576 | tf_op jit(solution)/shard_map/all_to_all | solution.py:72
  245.6 0.7 reshape.240
  246.9 0.7 copy.139
  247.6 1.8 reshape.241
  249.3 4.9 all-to-all-start.3
  254.3 28.9 %reshape.204 = f32[32,8,4,64,64]{4,3,2,1,0:T(8,128)} reshape(f32[32,8,4,4096]{3,2,1,0:T(4,128)} %param.28) | data formatting | bytes 33554432 | tf_op jit(solution)/shard_map/reshape | solution.py:78
  283.7 2.1 reduce.8
  285.8 0.7 reshape.242
  287.3 1.2 convolution_bitcast_fusion.1
  288.5 32.6 %fusion.303 = f32[32,8,4,1,64]{4,3,2,1,0:T(1,128)S(1)} fusion(f32[32,8,4,64,64]{4,3,2,1,0:T(8,128)} %reshape.204, f32[64,32,8,4,1]{0,1,3,2,4:T(8,128)S(1)} %convolution_bitcast_fusion.1), kind=kOutput, calls=%fused_computation.378 | convolution fusion | flops 50331648 | bytes 17301504 | tf_op jit(solution)/shard_map/ojlk,jlkoq->qjlk/dot_general | solution.py:79
  321.2 1.2 fusion.293
  323.2 12.7 %all_to_all.92 = bf16[4,2,16384]{2,1,0:T(2,128)(2,1)S(1)} all-to-all(bf16[4,2,16384]{2,1,0:T(2,128)(2,1)S(1)} %reshape.243), channel_id=1, replica_groups=mesh['gx'=4,'gy'=8] {'gx'}, dimensions={0} | all-to-all | bytes 524288 | tf_op jit(solution)/shard_map/all_to_all | solution.py:81
  336.3 1.0 fusion.289
  337.4 0.8 copy.138
  338.2 0.7 reshape.245
  338.9 12.3 %all_to_all.93 = bf16[8,2,16384]{2,1,0:T(2,128)(2,1)S(1)} all-to-all(bf16[8,2,16384]{2,1,0:T(2,128)(2,1)S(1)} %reshape.245), channel_id=1, replica_groups=mesh['gx'=4,'gy'=8] {'gy'}, dimensions={0} | all-to-all | bytes 1048576 | tf_op jit(solution)/shard_map/all_to_all | solution.py:85
  352.3 2.4 fusion.323
  354.8 14.5 %fusion.279 = bf16[64,16,8,64]{3,0,2,1:T(8,128)(2,1)S(1)} fusion(f32[64,16,8,64]{3,0,2,1:T(8,128)S(1)} %fusion.323, f32[64,16,8,64]{3,0,2,1:T(8,128)} %copy-done.1, f32[64]{0:T(128)S(1)} %copy-done.11, f32[64,64]{1,0:T(8,128)S(1)} %copy-done), kind=kOutput, calls=%fused_computation.339 | convolution fusion | flops 437780480 | bytes 5259520 | tf_op jit(solution)/shard_map/oxyz,oq->qxyz/dot_general | solution.py:90
  369.3 1.4 fusion.290
  370.7 1.0 copy.78
  371.7 3.5 all-to-all-start.6
  375.2 9.6 %all-to-all-done.6 = bf16[8,4,64,128]{3,1,2,0:T(4,128)(2,1)S(1)} async-done(((bf16[8,4,64,128]{3,1,2,0:T(4,128)(2,1)}), bf16[8,4,64,128]{3,1,2,0:T(4,128)(2,1)S(1)}, u32[]{:S(2)}, u32[]{:S(2)}) %all-to-all-start.6) | async-done | bytes 524320 | tf_op jit(solution)/shard_map/all_to_all | solution.py:169
  385.0 1.0 fusion.294
  386.0 174.1 %while.25 = (s32[]{:T(128)}, f32[2,8,128]{2,1,0:T(8,128)}, bf16[64,64]{1,0:T(8,128)(2,1)S(1)}, bf16[2,8,64,128]{3,1,0,2:T(8,128)(2,1)}, bf16[2,8,3,128]{3,1,2,0:...) while((s32[]{:T(128)}, f32[2,8,128]{2,1,0:T(8,128)}, ...), condition=%wide.region_5.6_spmd, body=%wide.region_4.5_spmd.sunk | while | flops 1684092928 | bytes 22110176 | solution.py:65
  386.2 0.7 bitcast_convert_fusion.8
  387.2 0.8 slice_bitcast_fusion.9
  388.1 0.9 constant_dynamic-slice_fusion.2
  389.1 2.2 multiply_convert_fusion.9
  391.3 80.4 %fusion.380 = f32[8,64,128]{2,1,0:T(8,128)S(1)} fusion(f32[8,128,128]{2,1,0:T(8,128)S(1)} %get-tuple-element.455, f32[64]{0:T(128)S(1)} %get-tuple-element.510, f32[8,128,64]{1,2,0:T(8,128)S(1)} %broadcast_multiply_fusion.5, f32[64]{0:T(128)S(1)} %get-tuple-element.458, f32[8,128,128]{2,1,0:T(8,128)S(1)} %get-tuple-element.459, ...), kind=kOutput, calls=%fused_computation.27.clone.3 | convolution fusion | flops 1669332992 | bytes 10486528 | tf_op jit(solution)/shard_map/while/body/eval_jaxpr/bcph,bcho->bop/dot_general | solution.py:52
  471.7 0.8 fusion.381
  473.1 0.7 bitcast_convert_fusion.8
  474.1 0.8 slice_bitcast_fusion.9
  475.0 0.9 constant_dynamic-slice_fusion.2
  476.0 2.2 multiply_convert_fusion.9
  478.3 80.4 %fusion.380 = f32[8,64,128]{2,1,0:T(8,128)S(1)} fusion(f32[8,128,128]{2,1,0:T(8,128)S(1)} %get-tuple-element.455, f32[64]{0:T(128)S(1)} %get-tuple-element.510, f32[8,128,64]{1,2,0:T(8,128)S(1)} %broadcast_multiply_fusion.5, f32[64]{0:T(128)S(1)} %get-tuple-element.458, f32[8,128,128]{2,1,0:T(8,128)S(1)} %get-tuple-element.459, ...), kind=kOutput, calls=%fused_computation.27.clone.3 | convolution fusion | flops 1669332992 | bytes 10486528 | tf_op jit(solution)/shard_map/while/body/eval_jaxpr/bcph,bcho->bop/dot_general | solution.py:52
  558.6 0.8 fusion.381
  (85 shorter events, 9.9 us)
Async XLA Ops:
  0.0 354.7 %copy-start = (f32[64,64]{1,0:T(8,128)S(1)}, f32[64,64]{1,0:T(8,128)}, u32[]{:S(2)}) copy-start(f32[64,64]{1,0:T(8,128)} %param.29) | copy-start | bytes 49156
  2.3 0.6 copy-start.7
  4.4 189.3 %all-to-all-start = ((f32[8,1,4]{2,1,0:T(1,128)}), f32[8,1,4]{2,1,0:T(1,128)}, u32[]{:S(2)}, u32[]{:S(2)}) async-start(f32[8,1,4]{2,1,0:T(1,128)} %bitcast.37), calls=%async_computation | async-start | bytes 8192 | tf_op jit(solution)/shard_map/all_to_all | solution.py:154
  11.5 179.2 %copy-start.6 = (s32[8,4]{0,1:T(4,128)S(1)}, s32[8,4]{0,1:T(4,128)}, u32[]{:S(2)}) copy-start(s32[8,4]{0,1:T(4,128)} %multiply_add_fusion) | copy-start | bytes 388
  11.5 179.2 %copy-start.8 = (s32[16]{0:T(128)S(1)}, s32[16]{0:T(128)}, u32[]{:S(2)}) copy-start(s32[16]{0:T(128)} %copy-done.7) | copy-start | bytes 196
  14.1 86.1 %copy-start.2 = (f32[2,8,64,128]{3,2,1,0:T(8,128)S(1)}, f32[2,8,64,128]{3,2,1,0:T(8,128)}, u32[]{:S(2)}) copy-start(f32[2,8,64,128]{3,2,1,0:T(8,128)} %get-tuple-element.471) | copy-start | bytes 1572868 | tf_op jit(solution)/shard_map/while
  100.2 0.8 copy-start.3
  103.6 86.1 %copy-start.2 = (f32[2,8,64,128]{3,2,1,0:T(8,128)S(1)}, f32[2,8,64,128]{3,2,1,0:T(8,128)}, u32[]{:S(2)}) copy-start(f32[2,8,64,128]{3,2,1,0:T(8,128)} %get-tuple-element.471) | copy-start | bytes 1572868 | tf_op jit(solution)/shard_map/while
  189.7 0.8 copy-start.3
  193.7 19.6 %all-to-all-start.1 = ((f32[8,4,64,128]{3,2,1,0:T(8,128)}), f32[8,4,64,128]{3,2,1,0:T(8,128)S(1)}, u32[]{:S(2)}, u32[]{:S(2)}) async-start(f32[8,4,64,128]{3,2,1,0:T(8,128)} %copy.61), calls=%async_computation.1 | async-start | bytes 2097152 | tf_op jit(solution)/shard_map/all_to_all | solution.py:147
  218.7 2.1 copy-start.1
  249.3 33.8 %all-to-all-start.3 = ((f32[4,1,32768]{2,1,0:T(1,128)}), f32[4,1,32768]{2,1,0:T(1,128)S(1)}, u32[]{:S(2)}, u32[]{:S(2)}) async-start(f32[4,1,32768]{2,1,0:T(1,128)} %reshape.241), calls=%async_computation.3 | async-start | bytes 1048576 | tf_op jit(solution)/shard_map/all_to_all | solution.py:76
  287.1 67.6 %copy-start.11 = (f32[64]{0:T(128)S(1)}, f32[64]{0:T(128)}, u32[]{:S(2)}) copy-start(f32[64]{0:T(128)} %param.30) | copy-start | bytes 772
  354.7 31.3 %copy-start.4 = (bf16[64,64]{1,0:T(8,128)(2,1)S(1)}, bf16[64,64]{1,0:T(8,128)(2,1)}, u32[]{:S(2)}) copy-start(bf16[64,64]{1,0:T(8,128)(2,1)} %param.27) | copy-start | bytes 24580
  354.7 31.3 %copy-start.12 = (f32[64]{0:T(128)S(1)}, f32[64]{0:T(128)}, u32[]{:S(2)}) copy-start(f32[64]{0:T(128)} %param.26) | copy-start | bytes 772
  371.7 13.1 %all-to-all-start.6 = ((bf16[8,4,64,128]{3,1,2,0:T(4,128)(2,1)}), bf16[8,4,64,128]{3,1,2,0:T(4,128)(2,1)S(1)}, u32[]{:S(2)}, u32[]{:S(2)}) async-start(bf16[8,4,64,128]{3,1,2,0:T(4,128)(2,1)} %copy.78), calls=%async_computation.6 | async-start | bytes 1048576 | tf_op jit(solution)/shard_map/all_to_all | solution.py:169
  391.3 80.4 %copy-start.13 = (f32[64]{0:T(128)S(1)}, f32[64]{0:T(128)}, u32[]{:S(2)}) copy-start(f32[64]{0:T(128)} %get-tuple-element.511) | copy-start | bytes 772 | tf_op jit(solution)/shard_map/while
  391.3 81.2 %copy-start.9 = (f32[2,8,128]{2,1,0:T(8,128)S(1)}, f32[2,8,128]{2,1,0:T(8,128)}, u32[]{:S(2)}) copy-start(f32[2,8,128]{2,1,0:T(8,128)} %get-tuple-element.496) | copy-start | bytes 24580 | tf_op jit(solution)/shard_map/while
  391.3 81.8 %copy-start.5 = (bf16[64,64]{1,0:T(8,128)(2,1)S(1)}, bf16[64,64]{1,0:T(8,128)(2,1)}, u32[]{:S(2)}) copy-start(bf16[64,64]{1,0:T(8,128)(2,1)} %get-tuple-element.525) | copy-start | bytes 24580 | tf_op jit(solution)/shard_map/while
  472.5 0.6 copy-start.10
  478.2 80.4 %copy-start.13 = (f32[64]{0:T(128)S(1)}, f32[64]{0:T(128)}, u32[]{:S(2)}) copy-start(f32[64]{0:T(128)} %get-tuple-element.511) | copy-start | bytes 772 | tf_op jit(solution)/shard_map/while
  478.2 81.2 %copy-start.9 = (f32[2,8,128]{2,1,0:T(8,128)S(1)}, f32[2,8,128]{2,1,0:T(8,128)}, u32[]{:S(2)}) copy-start(f32[2,8,128]{2,1,0:T(8,128)} %get-tuple-element.496) | copy-start | bytes 24580 | tf_op jit(solution)/shard_map/while
  478.3 81.8 %copy-start.5 = (bf16[64,64]{1,0:T(8,128)(2,1)S(1)}, bf16[64,64]{1,0:T(8,128)(2,1)}, u32[]{:S(2)}) copy-start(bf16[64,64]{1,0:T(8,128)(2,1)} %get-tuple-element.525) | copy-start | bytes 24580 | tf_op jit(solution)/shard_map/while
  559.5 0.6 copy-start.10
where the time goes:
time: 571 us; the launch traced here: 560 us
  matrix products  408 us (71%)
  local copies, waits for them, and re-layouts  56.7 us (10%)
  blocking collectives  37.1 us (6%)
  waiting for transfers between devices  22.9 us (4%)
  starting transfers between devices  17.8 us (3%)
  other arithmetic  16.8 us (3%)
    dot_general x2, matrix products, encode(): jnp.einsum('bcph,bop->bcho', weighted, feats, preferred_element_type=jnp....  172 us
    dot_general x2, matrix products, decode(): jnp.einsum('bcph,bcho->bop', weighted, folded, preferred_element_type=jnp...  161 us
    dot_general x1, matrix products, fourier(): jnp.einsum('ojlk,jlkoq->qjlk', spectrum, mode_weight, precision=highest)  32.6 us
    reshape x1, local copies, waits for them, and re-layouts, fourier(): spec_weight.reshape(spec_weight.shape[:3] + (channels, channels))  28.9 us
    dot_general x1, matrix products, fourier(): jnp.einsum('oxyz,oq->qxyz', pencil, local_weight, precision=highest)  14.5 us
    all_to_all x1, waiting for transfers between devices, local(): lax.all_to_all(send_terms.reshape(cols_count, capacity, channels, tile_ce...  13.3 us
    all_to_all x1, blocking collectives, fourier(): lax.all_to_all(returned.astype(jnp.bfloat16), 'gx', split_axis=1, concat_...  12.7 us
    all_to_all x1, blocking collectives, fourier(): lax.all_to_all(returned.astype(jnp.bfloat16), 'gy', split_axis=2, concat_...  12.3 us
  transfers between devices with their start and end apart: 4, of which 2 were waited for; matrix products, arithmetic and copies ran while one was open for 38% of the time, Pallas kernels for 0%

commit v1 on v0

--- a/solution.py
+++ b/solution.py
@@ -2,11 +2,19 @@
 import jax.numpy as jnp
 from jax import lax
 from jax.sharding import PartitionSpec as P
+from jax.lax import all_to_all, axis_size
 
 G = 64
 M = 32
 kernel_spread = 2.0
 highest = lax.Precision.HIGHEST
+
+
+def divide_turns(packet, out_dim, array_axis):
+    local_next = jnp.split(packet, axis_size("gy"), axis=out_dim)
+    moved = jnp.stack(local_next)
+    newest = jnp.concatenate(all_to_all(moved, "gy", 0, 0), axis=array_axis)
+    return newest
 
 
 def real_basis(length, modes):
@@ -82,9 +90,7 @@
         returned.astype(jnp.bfloat16), "gx", split_axis=1, concat_axis=2, tiled=True
     ).astype(returned.dtype)
     returned = jnp.einsum("oxlk,ly->oxyk", returned, table, precision=highest)
-    returned = lax.all_to_all(
-        returned.astype(jnp.bfloat16), "gy", split_axis=2, concat_axis=3, tiled=True
-    ).astype(returned.dtype)
+    returned = divide_turns(returned.astype(jnp.bfloat16), 2, 3).astype(returned.dtype)
     returned = jnp.einsum("oxyk,kz->oxyz", returned, table, precision=highest)
     local_term = (
         jnp.einsum("oxyz,oq->qxyz", pencil, local_weight, precision=highest)

time: 571 us -> 570 us (level)
  no operation moved by 1% of the time
where the time goes in v1:
time: 570 us; the launch traced here: 560 us
  matrix products  408 us (72%)
  local copies, waits for them, and re-layouts  55.9 us (10%)
  blocking collectives  37.2 us (7%)
  waiting for transfers between devices  22.9 us (4%)
  starting transfers between devices  17.8 us (3%)
  other arithmetic  16.8 us (3%)
    dot_general x2, matrix products, encode(): jnp.einsum('bcph,bop->bcho', weighted, feats, preferred_element_type=jnp....  172 us
    dot_general x2, matrix products, decode(): jnp.einsum('bcph,bcho->bop', weighted, folded, preferred_element_type=jnp...  161 us
    dot_general x1, matrix products, fourier(): jnp.einsum('ojlk,jlkoq->qjlk', spectrum, mode_weight, precision=highest)  32.6 us
    reshape x1, local copies, waits for them, and re-layouts, fourier(): spec_weight.reshape(spec_weight.shape[:3] + (channels, channels))  28.9 us
    dot_general x1, matrix products, fourier(): jnp.einsum('oxyz,oq->qxyz', pencil, local_weight, precision=highest)  14.5 us
    all_to_all x1, waiting for transfers between devices, local(): lax.all_to_all(send_terms.reshape(cols_count, capacity, channels, tile_ce...  13.3 us
    all_to_all x1, blocking collectives, fourier(): lax.all_to_all(returned.astype(jnp.bfloat16), 'gx', split_axis=1, concat_...  12.7 us
    all_to_all x1, blocking collectives, divide_turns(): newest = jnp.concatenate(all_to_all(moved, 'gy', 0, 0), axis=array_axis)  12.3 us
  transfers between devices with their start and end apart: 4, of which 2 were waited for; matrix products, arithmetic and copies ran while one was open for 38% of the time, Pallas kernels for 0%

profile of v1, /device:TPU:0, one launch (start us, length us, event | category | flops | bytes accessed | tf_op | source)
XLA Modules:
  0.0 559.7 jit_solution(15994533511022582742)
XLA Ops:
  0.0 0.7 fusion.326
  0.8 0.8 select_reduce_fusion
  1.6 0.7 multiply_add_fusion.1
  2.8 0.8 convolution_bitcast_fusion.2
  3.7 0.7 all_to_all.54
  4.4 5.2 all-to-all-start
  10.1 1.3 copy.59
  11.5 179.2 %while.24 = (s32[]{:T(128)}, f32[2,8,64,128]{3,2,1,0:T(8,128)}, bf16[2,8,3,128]{3,1,2,0:T(8,128)(2,1)}, f32[3,64]{1,0:T(4,128)}, f32[64]{0:T(128)}, /*index=5*/b...) while((s32[]{:T(128)}, f32[2,8,64,128]{3,2,1,0:T(8,128)}, bf16[2,8,3,128]{3,1,2,0:T(8,128)(2,1)}, ...), condition=%wide.region_3.4_spmd, body=%wide.region_2.3_spmd.sunk | while | flops 1678981120 | bytes 9416085 | solution.py:73
  11.5 0.7 bitcast_convert_fusion.7
  12.5 0.8 slice_bitcast_fusion.16
  13.3 0.7 bitcast_convert_fusion.6
  14.1 85.9 %multiply_reduce_fusion.2 = f32[64,8,128]{0,2,1:T(8,128)S(1)} fusion(f32[64,64]{0,1:T(8,128)S(1)} %bitcast_convert_fusion.6, f32[8,128,128]{2,1,0:T(8,128)S(1)} %get-tuple-element.435, f32[64]{0:T(128)} %get-tuple-element.482, f32[8,128,64]{1,2,0:T(8,128)S(1)} %broadcast_multiply_fusion.4, f32[64]{0:T(128)S(1)} %get-tuple-element.438, ...), kind=kOutput, calls=%fused_computation.219.clone.3 | convolution fusion | flops 1677656064 | bytes 2246144 | tf_op jit(solution)/shard_map/while/body/eval_jaxpr/bcph,bop->bcho/dot_general | solution.py:49
  100.2 0.8 copy-done.3
  101.0 0.7 bitcast_convert_fusion.7
  102.0 0.8 slice_bitcast_fusion.16
  102.9 0.7 bitcast_convert_fusion.6
  103.6 85.9 %multiply_reduce_fusion.2 = f32[64,8,128]{0,2,1:T(8,128)S(1)} fusion(f32[64,64]{0,1:T(8,128)S(1)} %bitcast_convert_fusion.6, f32[8,128,128]{2,1,0:T(8,128)S(1)} %get-tuple-element.435, f32[64]{0:T(128)} %get-tuple-element.482, f32[8,128,64]{1,2,0:T(8,128)S(1)} %broadcast_multiply_fusion.4, f32[64]{0:T(128)S(1)} %get-tuple-element.438, ...), kind=kOutput, calls=%fused_computation.219.clone.3 | convolution fusion | flops 1677656064 | bytes 2246144 | tf_op jit(solution)/shard_map/while/body/eval_jaxpr/bcph,bop->bcho/dot_general | solution.py:49
  189.7 0.8 copy-done.3
  190.7 1.8 fusion.302
  192.5 1.2 copy.61
  193.7 4.2 all-to-all-start.1
  198.6 1.3 reduce.5
  200.0 13.3 %all-to-all-done.1 = f32[8,4,64,128]{3,2,1,0:T(8,128)S(1)} async-done(((f32[8,4,64,128]{3,2,1,0:T(8,128)}), f32[8,4,64,128]{3,2,1,0:T(8,128)S(1)}, u32[]{:S(2)}, u32[]{:S(2)}) %all-to-all-start.1) | async-done | bytes 1048608 | tf_op jit(solution)/shard_map/all_to_all | solution.py:153
  213.3 1.8 copy.62
  215.1 3.5 fusion.319
  218.7 2.1 copy-done.1
  220.7 11.4 %convolution_convert_fusion.1 = bf16[64,16,8,32]{0,3,2,1:T(8,128)(2,1)S(1)} fusion(f32[64,16,8,64]{3,0,2,1:T(8,128)S(1)} %fusion.319, f32[16,64]{1,0:T(8,128)S(1)} %get-tuple-element.319, f32[16,64]{1,0:T(8,128)S(1)} %get-tuple-element.318), kind=kOutput, calls=%fused_computation.359 | convolution fusion | flops 201592832 | bytes 2629632 | tf_op jit(solution)/shard_map/oxyz,kz->oxyk/dot_general | solution.py:79
  232.6 0.9 reshape.247
  233.5 12.1 %all_to_all.78 = bf16[8,2,16384]{2,1,0:T(2,128)(2,1)S(1)} all-to-all(bf16[8,2,16384]{2,1,0:T(2,128)(2,1)S(1)} %reshape.247), channel_id=1, replica_groups=mesh['gx'=4,'gy'=8] {'gy'}, dimensions={0} | all-to-all | bytes 1048576 | tf_op jit(solution)/shard_map/all_to_all | solution.py:80
  245.6 0.7 reshape.248
  246.9 0.7 copy.139
  247.6 1.8 reshape.249
  249.3 4.9 all-to-all-start.3
  254.3 28.9 %reshape.210 = f32[32,8,4,64,64]{4,3,2,1,0:T(8,128)} reshape(f32[32,8,4,4096]{3,2,1,0:T(4,128)} %param.28) | data formatting | bytes 33554432 | tf_op jit(solution)/shard_map/reshape | solution.py:86
  283.7 2.1 reduce.8
  285.8 0.7 reshape.250
  287.3 1.2 convolution_bitcast_fusion.1
  288.5 32.6 %fusion.305 = f32[32,8,4,1,64]{4,3,2,1,0:T(1,128)S(1)} fusion(f32[32,8,4,64,64]{4,3,2,1,0:T(8,128)} %reshape.210, f32[64,32,8,4,1]{0,1,3,2,4:T(8,128)S(1)} %convolution_bitcast_fusion.1), kind=kOutput, calls=%fused_computation.380 | convolution fusion | flops 50331648 | bytes 17301504 | tf_op jit(solution)/shard_map/ojlk,jlkoq->qjlk/dot_general | solution.py:87
  321.2 1.2 fusion.293
  323.2 12.7 %all_to_all.79 = bf16[4,2,16384]{2,1,0:T(2,128)(2,1)S(1)} all-to-all(bf16[4,2,16384]{2,1,0:T(2,128)(2,1)S(1)} %reshape.251), channel_id=1, replica_groups=mesh['gx'=4,'gy'=8] {'gx'}, dimensions={0} | all-to-all | bytes 524288 | tf_op jit(solution)/shard_map/all_to_all | solution.py:89
  336.3 1.0 fusion.289
  337.7 0.7 reshape.253
  338.4 12.3 %all_to_all.80 = bf16[8,2,16384]{2,1,0:T(2,128)(2,1)S(1)} all-to-all(bf16[8,2,16384]{2,1,0:T(2,128)(2,1)S(1)} %reshape.253), channel_id=1, replica_groups=mesh['gx'=4,'gy'=8] {'gy'}, dimensions={0} | all-to-all | bytes 1048576 | tf_op jit(solution)/shard_map/all_to_all | solution.py:16
  350.8 0.7 reshape.254
  351.6 2.4 fusion.297
  354.0 14.5 %fusion.279 = bf16[64,16,8,64]{3,0,2,1:T(8,128)(2,1)S(1)} fusion(f32[64,16,8,64]{3,0,2,1:T(8,128)S(1)} %fusion.297, f32[64,16,8,64]{3,0,2,1:T(8,128)} %copy-done.1, f32[64]{0:T(128)S(1)} %copy-done.11, f32[64,64]{1,0:T(8,128)S(1)} %copy-done), kind=kOutput, calls=%fused_computation.339 | convolution fusion | flops 437780480 | bytes 5259520 | tf_op jit(solution)/shard_map/oxyz,oq->qxyz/dot_general | solution.py:96
  368.6 1.4 fusion.290
  369.9 1.0 copy.78
  370.9 3.5 all-to-all-start.6
  374.5 9.6 %all-to-all-done.6 = bf16[8,4,64,128]{3,1,2,0:T(4,128)(2,1)S(1)} async-done(((bf16[8,4,64,128]{3,1,2,0:T(4,128)(2,1)}), bf16[8,4,64,128]{3,1,2,0:T(4,128)(2,1)S(1)}, u32[]{:S(2)}, u32[]{:S(2)}) %all-to-all-start.6) | async-done | bytes 524320 | tf_op jit(solution)/shard_map/all_to_all | solution.py:175
  384.3 1.0 fusion.294
  385.3 174.1 %while.25 = (s32[]{:T(128)}, f32[2,8,128]{2,1,0:T(8,128)}, bf16[64,64]{1,0:T(8,128)(2,1)S(1)}, bf16[2,8,64,128]{3,1,0,2:T(8,128)(2,1)}, bf16[2,8,3,128]{3,1,2,0:...) while((s32[]{:T(128)}, f32[2,8,128]{2,1,0:T(8,128)}, ...), condition=%wide.region_5.6_spmd, body=%wide.region_4.5_spmd.sunk | while | flops 1684092928 | bytes 22110176 | solution.py:73
  385.5 0.7 bitcast_convert_fusion.8
  386.5 0.8 slice_bitcast_fusion.17
  387.3 0.9 constant_dynamic-slice_fusion.2
  388.3 2.2 multiply_convert_fusion.9
  390.6 80.4 %fusion.388 = f32[8,64,128]{2,1,0:T(8,128)S(1)} fusion(f32[8,128,128]{2,1,0:T(8,128)S(1)} %get-tuple-element.455, f32[64]{0:T(128)S(1)} %get-tuple-element.510, f32[8,128,64]{1,2,0:T(8,128)S(1)} %broadcast_multiply_fusion.5, f32[64]{0:T(128)S(1)} %get-tuple-element.458, f32[8,128,128]{2,1,0:T(8,128)S(1)} %get-tuple-element.459, ...), kind=kOutput, calls=%fused_computation.27.clone.3 | convolution fusion | flops 1669332992 | bytes 10486528 | tf_op jit(solution)/shard_map/while/body/eval_jaxpr/bcph,bcho->bop/dot_general | solution.py:60
  471.0 0.8 fusion.389
  472.4 0.7 bitcast_convert_fusion.8
  473.4 0.8 slice_bitcast_fusion.17
  474.3 0.9 constant_dynamic-slice_fusion.2
  475.3 2.2 multiply_convert_fusion.9
  477.5 80.4 %fusion.388 = f32[8,64,128]{2,1,0:T(8,128)S(1)} fusion(f32[8,128,128]{2,1,0:T(8,128)S(1)} %get-tuple-element.455, f32[64]{0:T(128)S(1)} %get-tuple-element.510, f32[8,128,64]{1,2,0:T(8,128)S(1)} %broadcast_multiply_fusion.5, f32[64]{0:T(128)S(1)} %get-tuple-element.458, f32[8,128,128]{2,1,0:T(8,128)S(1)} %get-tuple-element.459, ...), kind=kOutput, calls=%fused_computation.27.clone.3 | convolution fusion | flops 1669332992 | bytes 10486528 | tf_op jit(solution)/shard_map/while/body/eval_jaxpr/bcph,bcho->bop/dot_general | solution.py:60
  557.9 0.8 fusion.389
  (93 shorter events, 9.3 us)
Async XLA Ops:
  0.0 354.0 %copy-start = (f32[64,64]{1,0:T(8,128)S(1)}, f32[64,64]{1,0:T(8,128)}, u32[]{:S(2)}) copy-start(f32[64,64]{1,0:T(8,128)} %param.29) | copy-start | bytes 49156
  2.3 0.6 copy-start.7
  4.4 189.3 %all-to-all-start = ((f32[8,1,4]{2,1,0:T(1,128)}), f32[8,1,4]{2,1,0:T(1,128)}, u32[]{:S(2)}, u32[]{:S(2)}) async-start(f32[8,1,4]{2,1,0:T(1,128)} %bitcast.37), calls=%async_computation | async-start | bytes 8192 | tf_op jit(solution)/shard_map/all_to_all | solution.py:160
  11.5 179.2 %copy-start.6 = (s32[8,4]{0,1:T(4,128)S(1)}, s32[8,4]{0,1:T(4,128)}, u32[]{:S(2)}) copy-start(s32[8,4]{0,1:T(4,128)} %multiply_add_fusion) | copy-start | bytes 388
  11.5 179.2 %copy-start.8 = (s32[16]{0:T(128)S(1)}, s32[16]{0:T(128)}, u32[]{:S(2)}) copy-start(s32[16]{0:T(128)} %copy-done.7) | copy-start | bytes 196
  14.1 86.1 %copy-start.2 = (f32[2,8,64,128]{3,2,1,0:T(8,128)S(1)}, f32[2,8,64,128]{3,2,1,0:T(8,128)}, u32[]{:S(2)}) copy-start(f32[2,8,64,128]{3,2,1,0:T(8,128)} %get-tuple-element.471) | copy-start | bytes 1572868 | tf_op jit(solution)/shard_map/while
  100.2 0.8 copy-start.3
  103.6 86.1 %copy-start.2 = (f32[2,8,64,128]{3,2,1,0:T(8,128)S(1)}, f32[2,8,64,128]{3,2,1,0:T(8,128)}, u32[]{:S(2)}) copy-start(f32[2,8,64,128]{3,2,1,0:T(8,128)} %get-tuple-element.471) | copy-start | bytes 1572868 | tf_op jit(solution)/shard_map/while
  189.7 0.8 copy-start.3
  193.7 19.6 %all-to-all-start.1 = ((f32[8,4,64,128]{3,2,1,0:T(8,128)}), f32[8,4,64,128]{3,2,1,0:T(8,128)S(1)}, u32[]{:S(2)}, u32[]{:S(2)}) async-start(f32[8,4,64,128]{3,2,1,0:T(8,128)} %copy.61), calls=%async_computation.1 | async-start | bytes 2097152 | tf_op jit(solution)/shard_map/all_to_all | solution.py:153
  218.7 2.1 copy-start.1
  249.3 33.8 %all-to-all-start.3 = ((f32[4,1,32768]{2,1,0:T(1,128)}), f32[4,1,32768]{2,1,0:T(1,128)S(1)}, u32[]{:S(2)}, u32[]{:S(2)}) async-start(f32[4,1,32768]{2,1,0:T(1,128)} %reshape.249), calls=%async_computation.3 | async-start | bytes 1048576 | tf_op jit(solution)/shard_map/all_to_all | solution.py:84
  287.3 66.7 %copy-start.11 = (f32[64]{0:T(128)S(1)}, f32[64]{0:T(128)}, u32[]{:S(2)}) copy-start(f32[64]{0:T(128)} %param.30) | copy-start | bytes 772
  354.0 31.3 %copy-start.4 = (bf16[64,64]{1,0:T(8,128)(2,1)S(1)}, bf16[64,64]{1,0:T(8,128)(2,1)}, u32[]{:S(2)}) copy-start(bf16[64,64]{1,0:T(8,128)(2,1)} %param.27) | copy-start | bytes 24580
  354.0 31.3 %copy-start.12 = (f32[64]{0:T(128)S(1)}, f32[64]{0:T(128)}, u32[]{:S(2)}) copy-start(f32[64]{0:T(128)} %param.26) | copy-start | bytes 772
  370.9 13.1 %all-to-all-start.6 = ((bf16[8,4,64,128]{3,1,2,0:T(4,128)(2,1)}), bf16[8,4,64,128]{3,1,2,0:T(4,128)(2,1)S(1)}, u32[]{:S(2)}, u32[]{:S(2)}) async-start(bf16[8,4,64,128]{3,1,2,0:T(4,128)(2,1)} %copy.78), calls=%async_computation.6 | async-start | bytes 1048576 | tf_op jit(solution)/shard_map/all_to_all | solution.py:175
  390.5 80.4 %copy-start.13 = (f32[64]{0:T(128)S(1)}, f32[64]{0:T(128)}, u32[]{:S(2)}) copy-start(f32[64]{0:T(128)} %get-tuple-element.511) | copy-start | bytes 772 | tf_op jit(solution)/shard_map/while
  390.6 81.2 %copy-start.9 = (f32[2,8,128]{2,1,0:T(8,128)S(1)}, f32[2,8,128]{2,1,0:T(8,128)}, u32[]{:S(2)}) copy-start(f32[2,8,128]{2,1,0:T(8,128)} %get-tuple-element.496) | copy-start | bytes 24580 | tf_op jit(solution)/shard_map/while
  390.6 81.8 %copy-start.5 = (bf16[64,64]{1,0:T(8,128)(2,1)S(1)}, bf16[64,64]{1,0:T(8,128)(2,1)}, u32[]{:S(2)}) copy-start(bf16[64,64]{1,0:T(8,128)(2,1)} %get-tuple-element.525) | copy-start | bytes 24580 | tf_op jit(solution)/shard_map/while
  471.8 0.6 copy-start.10
  477.5 80.4 %copy-start.13 = (f32[64]{0:T(128)S(1)}, f32[64]{0:T(128)}, u32[]{:S(2)}) copy-start(f32[64]{0:T(128)} %get-tuple-element.511) | copy-start | bytes 772 | tf_op jit(solution)/shard_map/while
  477.5 81.2 %copy-start.9 = (f32[2,8,128]{2,1,0:T(8,128)S(1)}, f32[2,8,128]{2,1,0:T(8,128)}, u32[]{:S(2)}) copy-start(f32[2,8,128]{2,1,0:T(8,128)} %get-tuple-element.496) | copy-start | bytes 24580 | tf_op jit(solution)/shard_map/while
  477.5 81.8 %copy-start.5 = (bf16[64,64]{1,0:T(8,128)(2,1)S(1)}, bf16[64,64]{1,0:T(8,128)(2,1)}, u32[]{:S(2)}) copy-start(bf16[64,64]{1,0:T(8,128)(2,1)} %get-tuple-element.525) | copy-start | bytes 24580 | tf_op jit(solution)/shard_map/while
  558.7 0.6 copy-start.10
